TPU v7x, 128 devices: a whole 4x4x4 slice. The times are simulated.
128 devices in a mesh: section: 8 (over x, core), seq: 16 (over z, y).
Axes of the slice: x: 4, y: 4, z: 4, core: 2. Of those that a mesh axis runs over, the one named last changes fastest.
Arguments:
- residual: bfloat16 [8, 4096, 2048], P('section', 'seq'), may hold values from -6 to 6
- w_qkv: bfloat16 [8, 2048, 6144], P('section', 'seq'), may hold values from -0.125 to 0.125
- w_beta: bfloat16 [8, 2048, 16], P('section', 'seq'), may hold values from -0.125 to 0.125
- beta_bias: float32 [8, 16], P('section'), may hold values from -8 to 2
- norm_gain: float32 [8, 2048], P('section'), may hold values from 0.1 to 1.9
- out_gain: float32 [8, 128], P('section'), may hold values from 0.1 to 1.9
- state_in: float32 [8, 16, 128, 128], P('section'), may hold values from -6 to 6
- doc_start: int32 [2, 8], P(None, 'section'), may hold values from 0 to 64, as said below
Outputs:
- stream_out: bfloat16 [8, 4096, 2048], P('section', 'seq')
Inputs may be any that keep to these rules, and one draw needn't show every extreme that they name: `doc_start`: 64 means no new document in that micro-batch.
All inputs are finite; a program needn't handle non-finite values.
Results may differ from a plain program's by a relative error of at most 0.03.
Values may be sent and summed in bfloat16 or wider, within the bound.
No kernel may reach another device: no remote copies, remote signals or barrier semaphores. Data moves between devices by JAX's collectives and lax.ppermute only.
A program may use at most 192 MiB of HBM per device.

v0:
```python
import jax
import jax.numpy as jnp
from jax import lax
from jax.sharding import PartitionSpec as P

HEADS = 16
HD = 128
GROUP = 64
TICKS = 2
FULL_PRECISION = lax.Precision.HIGHEST


def from_behind(value, axis, by):
    count = lax.axis_size(axis)
    pairs = [(i, i + by) for i in range(count) if 0 <= i + by < count]
    return lax.ppermute(value, axis, pairs)


def from_root(value, axis, source):
    kept = jnp.where(lax.axis_index(axis) == source, value, 0).astype(value.dtype)
    return lax.psum(kept, axis)


def passed_along(value, axis, by):
    count = lax.axis_size(axis)
    return lax.ppermute(value, axis, [(i, (i + by) % count) for i in range(count)])


def unit_norm(projected):
    return projected * lax.rsqrt(jnp.sum(projected * projected, axis=-1, keepdims=True) + 1e-06)


def block_solve(key_rows, values, beta_rows):
    block_len = key_rows.shape[-2]
    intersections = jnp.einsum("ghik,ghjk->ghij", key_rows, key_rows, precision=FULL_PRECISION)
    system = jnp.tril(intersections * beta_rows[..., :, None], -1) + jnp.eye(
        block_len, dtype=jnp.float32
    )
    right_side = jnp.concatenate(
        [values * beta_rows[..., None], key_rows * beta_rows[..., None]], axis=-1
    )
    solved = lax.linalg.triangular_solve(
        system, right_side, left_side=True, lower=True, unit_diagonal=True
    )
    head_width = values.shape[-1]
    return (solved[..., :head_width], solved[..., head_width:])


def prepare(stream, weight_qkv, weight_beta, head_bias, in_gain):
    row_count = stream.shape[0]
    widened = stream.astype(jnp.float32)
    normed = (
        widened * lax.rsqrt(jnp.mean(widened * widened, axis=-1, keepdims=True) + 1e-05) * in_gain
    ).astype(jnp.bfloat16)
    projected = jnp.dot(normed, weight_qkv, preferred_element_type=jnp.float32).reshape(
        row_count, 3, HEADS, HD
    )
    queries = unit_norm(projected[:, 0]).astype(jnp.bfloat16)
    key_rows = unit_norm(projected[:, 1]).astype(jnp.bfloat16)
    values = projected[:, 2].astype(jnp.bfloat16)
    beta_rows = jax.nn.sigmoid(
        jnp.dot(normed, weight_beta, preferred_element_type=jnp.float32) + head_bias
    )
    blocks = row_count // GROUP

    def to_blocks(tensor):
        return tensor.astype(jnp.float32).reshape(blocks, GROUP, HEADS, HD).transpose(0, 2, 1, 3)

    beta_blk = beta_rows.reshape(blocks, GROUP, HEADS).transpose(0, 2, 1)
    key_block = to_blocks(key_rows)
    inject, weights = block_solve(key_block, to_blocks(values), beta_blk)
    return (to_blocks(queries), key_block, inject, weights, widened)


def run_blocks(queries, key_rows, inject, weights, current_state, doc_block, first_block):
    block_count = queries.shape[0]
    block_len = queries.shape[2]
    causal = jnp.tril(jnp.ones((block_len, block_len), jnp.float32))

    def run_advance(current_state, pieces):
        query_block, key_block, inject_block, weight_block, block_index = pieces
        current_state = jnp.where(
            block_index == doc_block, jnp.zeros_like(current_state), current_state
        )
        delta_values = inject_block - jnp.einsum(
            "jxy,jyu->jxu", weight_block, current_state, precision=FULL_PRECISION
        )
        attention_scores = (
            jnp.einsum("hik,hjk->hij", query_block, key_block, precision=FULL_PRECISION) * causal
        )
        block_result = jnp.einsum(
            "jxy,jyu->jxu", query_block, current_state, precision=FULL_PRECISION
        ) + jnp.einsum("ucd,udo->uco", attention_scores, delta_values, precision=FULL_PRECISION)
        current_state = current_state + jnp.einsum(
            "plq,plw->pqw", key_block, delta_values, precision=FULL_PRECISION
        )
        return (current_state, block_result)

    block_ids = first_block + jnp.arange(block_count, dtype=jnp.int32)
    return lax.scan(run_advance, current_state, (queries, key_rows, inject, weights, block_ids))


def transitions(key_rows, inject, weights, doc_block, first_block):
    head_count = key_rows.shape[1]
    head_width = key_rows.shape[3]
    block_count = key_rows.shape[0]
    identity = jnp.broadcast_to(
        jnp.eye(head_width, dtype=jnp.float32), (head_count, head_width, head_width)
    )

    def transitions_advance(maps, pieces):
        decay_matrix, start_offset = maps
        key_block, inject_block, weight_block, block_index = pieces
        keep_flag = block_index != doc_block
        decay_matrix = jnp.where(keep_flag, decay_matrix, jnp.zeros_like(decay_matrix))
        start_offset = jnp.where(keep_flag, start_offset, jnp.zeros_like(start_offset))
        decay_matrix = decay_matrix - jnp.einsum(
            "plq,plw->pqw",
            key_block,
            jnp.einsum("jxy,jyu->jxu", weight_block, decay_matrix, precision=FULL_PRECISION),
            precision=FULL_PRECISION,
        )
        start_offset = start_offset + jnp.einsum(
            "plq,plw->pqw",
            key_block,
            inject_block
            - jnp.einsum("jxy,jyu->jxu", weight_block, start_offset, precision=FULL_PRECISION),
            precision=FULL_PRECISION,
        )
        return ((decay_matrix, start_offset), None)

    block_ids = first_block + jnp.arange(block_count, dtype=jnp.int32)
    maps, unused = lax.scan(
        transitions_advance,
        (identity, jnp.zeros_like(identity)),
        (key_rows, inject, weights, block_ids),
    )
    return maps


def apply_map(maps, given_state):
    return jnp.einsum("hij,hjk->hik", maps[0], given_state, precision=FULL_PRECISION) + maps[1]


def compose(earlier, latter):
    return (
        jnp.einsum("hij,hjk->hik", latter[0], earlier[0], precision=FULL_PRECISION),
        jnp.einsum("hij,hjk->hik", latter[0], earlier[1], precision=FULL_PRECISION) + latter[1],
    )


def finish(widened, block_result, head_gain):
    blocks = block_result.shape[0]
    mixed = block_result.transpose(0, 2, 1, 3).reshape(blocks * GROUP, HEADS, HD)
    mixed = mixed * lax.rsqrt(jnp.mean(mixed * mixed, axis=-1, keepdims=True) + 1e-05) * head_gain
    return (widened + mixed.reshape(blocks * GROUP, HEADS * HD)).astype(jnp.bfloat16)


def shards(residual, w_qkv, w_beta, beta_bias, norm_gain, out_gain, state_in, doc_start):
    weight_qkv, weight_beta = (
        lax.all_gather(w_qkv[0], "seq", axis=0, tiled=True),
        lax.all_gather(w_beta[0], "seq", axis=0, tiled=True),
    )
    seq_count = lax.axis_size("seq")
    position = lax.axis_index("seq")
    stream = residual[0]
    given_state = state_in[0]
    blocks = stream.shape[0] // GROUP
    first_block = position * blocks
    outputs = stream
    identity = jnp.broadcast_to(jnp.eye(HD, dtype=jnp.float32), (HEADS, HD, HD))
    empty_map = jnp.stack([identity, jnp.zeros_like(identity)])
    for tick_index in range(TICKS):
        doc_block = doc_start[tick_index, 0]
        queries, key_rows, inject, weights, widened = prepare(
            stream, weight_qkv, weight_beta, beta_bias[0], norm_gain[0]
        )
        maps = transitions(key_rows, inject, weights, doc_block, first_block)

        def hop_once(hop_index, carried_map):
            joined = compose((carried_map[0], carried_map[1]), maps)
            passed = from_behind(
                jnp.stack([joined[0], joined[1]]).astype(jnp.bfloat16), "seq", 1
            ).astype(jnp.float32)
            return jnp.where(position == 0, empty_map, passed)

        prefix_map = lax.fori_loop(0, seq_count - 1, hop_once, empty_map)
        prefix = (prefix_map[0], prefix_map[1])
        entry_state = apply_map(prefix, given_state)
        final_state, block_result = run_blocks(
            queries, key_rows, inject, weights, entry_state, doc_block, first_block
        )
        outputs = finish(widened, block_result, out_gain[0])
        if tick_index + 1 < TICKS:
            given_state = from_root(final_state.astype(jnp.bfloat16), "seq", seq_count - 1).astype(
                final_state.dtype
            )
            stream = passed_along(outputs, "section", 1)
    return outputs[None]


def solution(mesh):
    return jax.shard_map(
        shards,
        mesh=mesh,
        in_specs=(
            P("section", "seq", None),
            P("section", "seq", None),
            P("section", "seq", None),
            P("section", None),
            P("section", None),
            P("section", None),
            P("section", None, None, None),
            P(None, "section"),
        ),
        out_specs=P("section", "seq", None),
        check_vma=False,
    )
```

profile of v0, /device:TPU:34, one launch (start us, length us, event | category | flops | bytes accessed | tf_op | source)
XLA Modules:
  0.0 2081.2 jit_solution(3336317457587673220)
XLA Ops:
  7.3 24.4 %all-gather.1 = bf16[1,2048,16]{1,2,0:T(8,128)(2,1)S(1)} all-gather(bf16[1,128,16]{1,2,0:T(8,128)(2,1)} %param.24), channel_id=3, replica_groups=mesh['section'=8,'seq'=16] {'seq'}, dimensions={1}, use_global_device_ids=true | all-gather | bytes 69632 | tf_op jit(solution)/shard_map/all_gather | solution.py:162
  35.8 130.0 %all-gather.4.cloned.1.call-done = bf16[1,2048,6144]{2,1,0:T(8,128)(2,1)} async-done(((bf16[1,128,6144]{2,1,0:T(8,128)(2,1)}), bf16[1,2048,6144]{2,1,0:T(8,128)(2,1)}) %all-gather.4.cloned.1.call-update) | async-done | bytes 25165840 | tf_op jit(solution)/shard_map/all_gather | solution.py:161
  165.8 29.7 %copy.95 = bf16[6144,2048]{1,0:T(8,128)(2,1)} copy(bf16[6144,2048]{0,1:T(8,128)(2,1)} %bitcast.357) | data formatting | bytes 50331648 | tf_op jit(solution)/shard_map/dot_general | solution.py:55
  217.8 316.0 %custom-call.6 = f32[4,16,1,64,64]{3,4,2,1,0:T(8,128)} custom-call(f32[4,16,1,64,64]{4,3,2,1,0:T(8,128)} %add_bitcast_fusion.1), custom_call_target="InvertDiagBlocksLowerTriangular" | custom-call | tf_op jit(solution)/shard_map/triangular_solve/custom-call.1 | solution.py:42
  543.2 41.3 %while.80 = (s32[]{:T(128)}, f32[16,128,128]{2,1,0:T(8,128)S(1)}, f32[16,128,128]{2,1,0:T(8,128)S(1)}, s32[4]{0:T(128)S(1)}, s32[]{:T(128)}, /*index=5*/f32[4,16...) while((s32[]{:T(128)}, f32[16,128,128]{2,1,0:T(8,128)S(1)}, ...), condition=%wide.region_3.5_spmd.clone, body=%wide.region_2.4_spmd.clone.sunk | while | flops 807534592 | bytes 19400364 | solution.py:133
  584.6 464.3 %while.76 = (s32[]{:T(128)}, f32[2,16,128,128]{3,2,1,0:T(8,128)}, pred[]{:T(512)}, f32[16,128,128]{2,1,0:T(8,128)S(1)}, f32[16,128,128]{2,1,0:T(8,128)S(1)}, /*index=5*/f32[2,16,128,128]{3,2,1,0:T(8,128)}, s32[]{:T(128)}) while((s32[]{:T(128)}, f32[2,16,128,128]{3,2,1,0:T(8,128)}, pred[]{:T(512)}, f32[16,128,128]{2,1,0:T(8,128)S(1)}, ...), condition=%wide.region_5.7_spmd, body=%wide.region_4.6_spmd.sunk | while | flops 807665664 | bytes 26214544 | solution.py:187
  591.6 27.0 %collective-permute-done = bf16[2,16,128,128]{3,2,1,0:T(8,128)(2,1)} collective-permute-done((bf16[2,16,128,128]{3,2,1,0:T(8,128)(2,1)}, bf16[2,16,128,128]{3,2,1,0:T(8,128)(2,1)}, u32[]{:S(2)}, u32[]{:S(2)}) %collective-permute-start) | collective-permute-done | bytes 1048608 | tf_op jit(solution)/shard_map/while/body/eval_jaxpr/ppermute | solution.py:16
  628.4 26.4 %collective-permute-done = bf16[2,16,128,128]{3,2,1,0:T(8,128)(2,1)} collective-permute-done((bf16[2,16,128,128]{3,2,1,0:T(8,128)(2,1)}, bf16[2,16,128,128]{3,2,1,0:T(8,128)(2,1)}, u32[]{:S(2)}, u32[]{:S(2)}) %collective-permute-start) | collective-permute-done | bytes 1048608 | tf_op jit(solution)/shard_map/while/body/eval_jaxpr/ppermute | solution.py:16
  664.5 25.5 %collective-permute-done = bf16[2,16,128,128]{3,2,1,0:T(8,128)(2,1)} collective-permute-done((bf16[2,16,128,128]{3,2,1,0:T(8,128)(2,1)}, bf16[2,16,128,128]{3,2,1,0:T(8,128)(2,1)}, u32[]{:S(2)}, u32[]{:S(2)}) %collective-permute-start) | collective-permute-done | bytes 1048608 | tf_op jit(solution)/shard_map/while/body/eval_jaxpr/ppermute | solution.py:16
  699.7 24.6 %collective-permute-done = bf16[2,16,128,128]{3,2,1,0:T(8,128)(2,1)} collective-permute-done((bf16[2,16,128,128]{3,2,1,0:T(8,128)(2,1)}, bf16[2,16,128,128]{3,2,1,0:T(8,128)(2,1)}, u32[]{:S(2)}, u32[]{:S(2)}) %collective-permute-start) | collective-permute-done | bytes 1048608 | tf_op jit(solution)/shard_map/while/body/eval_jaxpr/ppermute | solution.py:16
  734.0 23.6 %collective-permute-done = bf16[2,16,128,128]{3,2,1,0:T(8,128)(2,1)} collective-permute-done((bf16[2,16,128,128]{3,2,1,0:T(8,128)(2,1)}, bf16[2,16,128,128]{3,2,1,0:T(8,128)(2,1)}, u32[]{:S(2)}, u32[]{:S(2)}) %collective-permute-start) | collective-permute-done | bytes 1048608 | tf_op jit(solution)/shard_map/while/body/eval_jaxpr/ppermute | solution.py:16
  767.3 22.7 %collective-permute-done = bf16[2,16,128,128]{3,2,1,0:T(8,128)(2,1)} collective-permute-done((bf16[2,16,128,128]{3,2,1,0:T(8,128)(2,1)}, bf16[2,16,128,128]{3,2,1,0:T(8,128)(2,1)}, u32[]{:S(2)}, u32[]{:S(2)}) %collective-permute-start) | collective-permute-done | bytes 1048608 | tf_op jit(solution)/shard_map/while/body/eval_jaxpr/ppermute | solution.py:16
  799.8 21.8 %collective-permute-done = bf16[2,16,128,128]{3,2,1,0:T(8,128)(2,1)} collective-permute-done((bf16[2,16,128,128]{3,2,1,0:T(8,128)(2,1)}, bf16[2,16,128,128]{3,2,1,0:T(8,128)(2,1)}, u32[]{:S(2)}, u32[]{:S(2)}) %collective-permute-start) | collective-permute-done | bytes 1048608 | tf_op jit(solution)/shard_map/while/body/eval_jaxpr/ppermute | solution.py:16
  1055.1 48.0 %while.78 = (s32[]{:T(128)}, f32[16,128,128]{2,1,0:T(8,128)S(1)}, f32[4,16,64,128]{3,2,1,0:T(8,128)}, s32[4]{0:T(128)S(1)}, s32[]{:T(128)}, /*index=5*/f32[4,16,...) while((s32[]{:T(128)}, f32[16,128,128]{2,1,0:T(8,128)S(1)}, ...), condition=%wide.region_8.10_spmd.clone, body=%wide.region_7.9_spmd.clone.sunk | while | flops 806690816 | bytes 19451036 | solution.py:100
  1161.5 316.2 %custom-call.7 = f32[4,16,1,64,64]{3,4,2,1,0:T(8,128)} custom-call(f32[4,16,1,64,64]{4,3,2,1,0:T(8,128)} %add_bitcast_fusion), custom_call_target="InvertDiagBlocksLowerTriangular" | custom-call | tf_op jit(solution)/shard_map/triangular_solve/custom-call.1 | solution.py:42
  1487.0 54.6 %while.81 = (s32[]{:T(128)}, f32[16,128,128]{2,1,0:T(8,128)S(1)}, f32[16,128,128]{2,1,0:T(8,128)}, s32[4]{0:T(128)S(1)}, s32[]{:T(128)}, /*index=5*/f32[4,16,64,...) while((s32[]{:T(128)}, f32[16,128,128]{2,1,0:T(8,128)S(1)}, ...), condition=%wide.region_13.15_spmd.clone, body=%wide.region_12.14_spmd.clone.sunk | while | flops 807534592 | bytes 19401408 | solution.py:133
  1545.3 471.8 %while.77 = (s32[]{:T(128)}, f32[2,16,128,128]{3,2,1,0:T(8,128)}, pred[]{:T(512)}, f32[16,128,128]{2,1,0:T(8,128)S(1)}, f32[16,128,128]{2,1,0:T(8,128)}, /*index=5*/f32[2,16,128,128]{3,2,1,0:T(8,128)S(1)}, s32[]{:T(128)}) while((s32[]{:T(128)}, f32[2,16,128,128]{3,2,1,0:T(8,128)}, pred[]{:T(512)}, f32[16,128,128]{2,1,0:T(8,128)S(1)}, ...), condition=%wide.region_15.17_spmd, body=%wide.region_14.16_spmd.sunk | while | flops 807665664 | bytes 22020240 | solution.py:187
  1553.4 26.6 %collective-permute-done.1 = bf16[2,16,128,128]{3,2,1,0:T(8,128)(2,1)} collective-permute-done((bf16[2,16,128,128]{3,2,1,0:T(8,128)(2,1)}, bf16[2,16,128,128]{3,2,1,0:T(8,128)(2,1)}, u32[]{:S(2)}, u32[]{:S(2)}) %collective-permute-start.1) | collective-permute-done | bytes 1048608 | tf_op jit(solution)/shard_map/while/body/eval_jaxpr/ppermute | solution.py:16
  1590.7 25.7 %collective-permute-done.1 = bf16[2,16,128,128]{3,2,1,0:T(8,128)(2,1)} collective-permute-done((bf16[2,16,128,128]{3,2,1,0:T(8,128)(2,1)}, bf16[2,16,128,128]{3,2,1,0:T(8,128)(2,1)}, u32[]{:S(2)}, u32[]{:S(2)}) %collective-permute-start.1) | collective-permute-done | bytes 1048608 | tf_op jit(solution)/shard_map/while/body/eval_jaxpr/ppermute | solution.py:16
  1627.1 24.8 %collective-permute-done.1 = bf16[2,16,128,128]{3,2,1,0:T(8,128)(2,1)} collective-permute-done((bf16[2,16,128,128]{3,2,1,0:T(8,128)(2,1)}, bf16[2,16,128,128]{3,2,1,0:T(8,128)(2,1)}, u32[]{:S(2)}, u32[]{:S(2)}) %collective-permute-start.1) | collective-permute-done | bytes 1048608 | tf_op jit(solution)/shard_map/while/body/eval_jaxpr/ppermute | solution.py:16
  1662.6 23.8 %collective-permute-done.1 = bf16[2,16,128,128]{3,2,1,0:T(8,128)(2,1)} collective-permute-done((bf16[2,16,128,128]{3,2,1,0:T(8,128)(2,1)}, bf16[2,16,128,128]{3,2,1,0:T(8,128)(2,1)}, u32[]{:S(2)}, u32[]{:S(2)}) %collective-permute-start.1) | collective-permute-done | bytes 1048608 | tf_op jit(solution)/shard_map/while/body/eval_jaxpr/ppermute | solution.py:16
  1697.2 22.9 %collective-permute-done.1 = bf16[2,16,128,128]{3,2,1,0:T(8,128)(2,1)} collective-permute-done((bf16[2,16,128,128]{3,2,1,0:T(8,128)(2,1)}, bf16[2,16,128,128]{3,2,1,0:T(8,128)(2,1)}, u32[]{:S(2)}, u32[]{:S(2)}) %collective-permute-start.1) | collective-permute-done | bytes 1048608 | tf_op jit(solution)/shard_map/while/body/eval_jaxpr/ppermute | solution.py:16
  1730.8 22.0 %collective-permute-done.1 = bf16[2,16,128,128]{3,2,1,0:T(8,128)(2,1)} collective-permute-done((bf16[2,16,128,128]{3,2,1,0:T(8,128)(2,1)}, bf16[2,16,128,128]{3,2,1,0:T(8,128)(2,1)}, u32[]{:S(2)}, u32[]{:S(2)}) %collective-permute-start.1) | collective-permute-done | bytes 1048608 | tf_op jit(solution)/shard_map/while/body/eval_jaxpr/ppermute | solution.py:16
  2021.2 44.4 %while.79 = (s32[]{:T(128)}, f32[16,128,128]{2,1,0:T(8,128)S(1)}, f32[4,16,64,128]{3,2,1,0:T(8,128)}, s32[4]{0:T(128)S(1)}, s32[]{:T(128)}, /*index=5*/f32[4,16,...) while((s32[]{:T(128)}, f32[16,128,128]{2,1,0:T(8,128)S(1)}, ...), condition=%wide.region_19.21_spmd.clone, body=%wide.region_18.20_spmd.clone.sunk | while | flops 806690816 | bytes 12109449 | solution.py:100
  (477 shorter events, 909.3 us)
Async XLA Ops:
  6.5 159.2 %all-gather.4.cloned.1.call-start = ((), (), s32[]{:S(2)}) async-start(), calls=%async_computation.1 | async-start | bytes 26738688 | tf_op jit(solution)/shard_map/all_gather | solution.py:161
  7.3 1538.0 %all-reduce.3.cloned.1.call-start = ((), (), s32[]{:S(2)}) async-start(), calls=%async_computation | async-start | bytes 1048576 | tf_op jit(solution)/shard_map/psum | solution.py:21
  589.4 29.2 %collective-permute-start = (bf16[2,16,128,128]{3,2,1,0:T(8,128)(2,1)}, bf16[2,16,128,128]{3,2,1,0:T(8,128)(2,1)}, u32[]{:S(2)}, u32[]{:S(2)}) collective-permute-start(bf16[2,16,128,128]{3,2,1,0:T(8,128)(2,1)} %pad_maximum_fusion.4), channel_id=1, source_target_pairs={{0,1},{1,2},{2,3},{3,4},{4,5},{5,6},{6,7},{7,8},{8,9},{9,10},{10,1... | collective-permute-start | bytes 3145736 | tf_op jit(solution)/shard_map/while/body/eval_jaxpr/ppermute | solution.py:16
  626.4 28.3 %collective-permute-start = (bf16[2,16,128,128]{3,2,1,0:T(8,128)(2,1)}, bf16[2,16,128,128]{3,2,1,0:T(8,128)(2,1)}, u32[]{:S(2)}, u32[]{:S(2)}) collective-permute-start(bf16[2,16,128,128]{3,2,1,0:T(8,128)(2,1)} %pad_maximum_fusion.4), channel_id=1, source_target_pairs={{0,1},{1,2},{2,3},{3,4},{4,5},{5,6},{6,7},{7,8},{8,9},{9,10},{10,1... | collective-permute-start | bytes 3145736 | tf_op jit(solution)/shard_map/while/body/eval_jaxpr/ppermute | solution.py:16
  662.6 27.4 %collective-permute-start = (bf16[2,16,128,128]{3,2,1,0:T(8,128)(2,1)}, bf16[2,16,128,128]{3,2,1,0:T(8,128)(2,1)}, u32[]{:S(2)}, u32[]{:S(2)}) collective-permute-start(bf16[2,16,128,128]{3,2,1,0:T(8,128)(2,1)} %pad_maximum_fusion.4), channel_id=1, source_target_pairs={{0,1},{1,2},{2,3},{3,4},{4,5},{5,6},{6,7},{7,8},{8,9},{9,10},{10,1... | collective-permute-start | bytes 3145736 | tf_op jit(solution)/shard_map/while/body/eval_jaxpr/ppermute | solution.py:16
  697.8 26.5 %collective-permute-start = (bf16[2,16,128,128]{3,2,1,0:T(8,128)(2,1)}, bf16[2,16,128,128]{3,2,1,0:T(8,128)(2,1)}, u32[]{:S(2)}, u32[]{:S(2)}) collective-permute-start(bf16[2,16,128,128]{3,2,1,0:T(8,128)(2,1)} %pad_maximum_fusion.4), channel_id=1, source_target_pairs={{0,1},{1,2},{2,3},{3,4},{4,5},{5,6},{6,7},{7,8},{8,9},{9,10},{10,1... | collective-permute-start | bytes 3145736 | tf_op jit(solution)/shard_map/while/body/eval_jaxpr/ppermute | solution.py:16
  732.0 25.6 %collective-permute-start = (bf16[2,16,128,128]{3,2,1,0:T(8,128)(2,1)}, bf16[2,16,128,128]{3,2,1,0:T(8,128)(2,1)}, u32[]{:S(2)}, u32[]{:S(2)}) collective-permute-start(bf16[2,16,128,128]{3,2,1,0:T(8,128)(2,1)} %pad_maximum_fusion.4), channel_id=1, source_target_pairs={{0,1},{1,2},{2,3},{3,4},{4,5},{5,6},{6,7},{7,8},{8,9},{9,10},{10,1... | collective-permute-start | bytes 3145736 | tf_op jit(solution)/shard_map/while/body/eval_jaxpr/ppermute | solution.py:16
  765.4 24.6 %collective-permute-start = (bf16[2,16,128,128]{3,2,1,0:T(8,128)(2,1)}, bf16[2,16,128,128]{3,2,1,0:T(8,128)(2,1)}, u32[]{:S(2)}, u32[]{:S(2)}) collective-permute-start(bf16[2,16,128,128]{3,2,1,0:T(8,128)(2,1)} %pad_maximum_fusion.4), channel_id=1, source_target_pairs={{0,1},{1,2},{2,3},{3,4},{4,5},{5,6},{6,7},{7,8},{8,9},{9,10},{10,1... | collective-permute-start | bytes 3145736 | tf_op jit(solution)/shard_map/while/body/eval_jaxpr/ppermute | solution.py:16
  797.8 23.7 %collective-permute-start = (bf16[2,16,128,128]{3,2,1,0:T(8,128)(2,1)}, bf16[2,16,128,128]{3,2,1,0:T(8,128)(2,1)}, u32[]{:S(2)}, u32[]{:S(2)}) collective-permute-start(bf16[2,16,128,128]{3,2,1,0:T(8,128)(2,1)} %pad_maximum_fusion.4), channel_id=1, source_target_pairs={{0,1},{1,2},{2,3},{3,4},{4,5},{5,6},{6,7},{7,8},{8,9},{9,10},{10,1... | collective-permute-start | bytes 3145736 | tf_op jit(solution)/shard_map/while/body/eval_jaxpr/ppermute | solution.py:16
  829.3 22.8 %collective-permute-start = (bf16[2,16,128,128]{3,2,1,0:T(8,128)(2,1)}, bf16[2,16,128,128]{3,2,1,0:T(8,128)(2,1)}, u32[]{:S(2)}, u32[]{:S(2)}) collective-permute-start(bf16[2,16,128,128]{3,2,1,0:T(8,128)(2,1)} %pad_maximum_fusion.4), channel_id=1, source_target_pairs={{0,1},{1,2},{2,3},{3,4},{4,5},{5,6},{6,7},{7,8},{8,9},{9,10},{10,1... | collective-permute-start | bytes 3145736 | tf_op jit(solution)/shard_map/while/body/eval_jaxpr/ppermute | solution.py:16
  859.9 21.9 %collective-permute-start = (bf16[2,16,128,128]{3,2,1,0:T(8,128)(2,1)}, bf16[2,16,128,128]{3,2,1,0:T(8,128)(2,1)}, u32[]{:S(2)}, u32[]{:S(2)}) collective-permute-start(bf16[2,16,128,128]{3,2,1,0:T(8,128)(2,1)} %pad_maximum_fusion.4), channel_id=1, source_target_pairs={{0,1},{1,2},{2,3},{3,4},{4,5},{5,6},{6,7},{7,8},{8,9},{9,10},{10,1... | collective-permute-start | bytes 3145736 | tf_op jit(solution)/shard_map/while/body/eval_jaxpr/ppermute | solution.py:16
  889.6 20.9 %collective-permute-start = (bf16[2,16,128,128]{3,2,1,0:T(8,128)(2,1)}, bf16[2,16,128,128]{3,2,1,0:T(8,128)(2,1)}, u32[]{:S(2)}, u32[]{:S(2)}) collective-permute-start(bf16[2,16,128,128]{3,2,1,0:T(8,128)(2,1)} %pad_maximum_fusion.4), channel_id=1, source_target_pairs={{0,1},{1,2},{2,3},{3,4},{4,5},{5,6},{6,7},{7,8},{8,9},{9,10},{10,1... | collective-permute-start | bytes 3145736 | tf_op jit(solution)/shard_map/while/body/eval_jaxpr/ppermute | solution.py:16
  918.3 20.0 collective-permute-start
  1551.5 28.5 %collective-permute-start.1 = (bf16[2,16,128,128]{3,2,1,0:T(8,128)(2,1)}, bf16[2,16,128,128]{3,2,1,0:T(8,128)(2,1)}, u32[]{:S(2)}, u32[]{:S(2)}) collective-permute-start(bf16[2,16,128,128]{3,2,1,0:T(8,128)(2,1)} %pad_maximum_fusion.5), channel_id=1, source_target_pairs={{0,1},{1,2},{2,3},{3,4},{4,5},{5,6},{6,7},{7,8},{8,9},{9,10},{10,1... | collective-permute-start | bytes 3145736 | tf_op jit(solution)/shard_map/while/body/eval_jaxpr/ppermute | solution.py:16
  1588.8 27.6 %collective-permute-start.1 = (bf16[2,16,128,128]{3,2,1,0:T(8,128)(2,1)}, bf16[2,16,128,128]{3,2,1,0:T(8,128)(2,1)}, u32[]{:S(2)}, u32[]{:S(2)}) collective-permute-start(bf16[2,16,128,128]{3,2,1,0:T(8,128)(2,1)} %pad_maximum_fusion.5), channel_id=1, source_target_pairs={{0,1},{1,2},{2,3},{3,4},{4,5},{5,6},{6,7},{7,8},{8,9},{9,10},{10,1... | collective-permute-start | bytes 3145736 | tf_op jit(solution)/shard_map/while/body/eval_jaxpr/ppermute | solution.py:16
  1625.2 26.7 %collective-permute-start.1 = (bf16[2,16,128,128]{3,2,1,0:T(8,128)(2,1)}, bf16[2,16,128,128]{3,2,1,0:T(8,128)(2,1)}, u32[]{:S(2)}, u32[]{:S(2)}) collective-permute-start(bf16[2,16,128,128]{3,2,1,0:T(8,128)(2,1)} %pad_maximum_fusion.5), channel_id=1, source_target_pairs={{0,1},{1,2},{2,3},{3,4},{4,5},{5,6},{6,7},{7,8},{8,9},{9,10},{10,1... | collective-permute-start | bytes 3145736 | tf_op jit(solution)/shard_map/while/body/eval_jaxpr/ppermute | solution.py:16
  1660.7 25.8 %collective-permute-start.1 = (bf16[2,16,128,128]{3,2,1,0:T(8,128)(2,1)}, bf16[2,16,128,128]{3,2,1,0:T(8,128)(2,1)}, u32[]{:S(2)}, u32[]{:S(2)}) collective-permute-start(bf16[2,16,128,128]{3,2,1,0:T(8,128)(2,1)} %pad_maximum_fusion.5), channel_id=1, source_target_pairs={{0,1},{1,2},{2,3},{3,4},{4,5},{5,6},{6,7},{7,8},{8,9},{9,10},{10,1... | collective-permute-start | bytes 3145736 | tf_op jit(solution)/shard_map/while/body/eval_jaxpr/ppermute | solution.py:16
  1695.3 24.8 %collective-permute-start.1 = (bf16[2,16,128,128]{3,2,1,0:T(8,128)(2,1)}, bf16[2,16,128,128]{3,2,1,0:T(8,128)(2,1)}, u32[]{:S(2)}, u32[]{:S(2)}) collective-permute-start(bf16[2,16,128,128]{3,2,1,0:T(8,128)(2,1)} %pad_maximum_fusion.5), channel_id=1, source_target_pairs={{0,1},{1,2},{2,3},{3,4},{4,5},{5,6},{6,7},{7,8},{8,9},{9,10},{10,1... | collective-permute-start | bytes 3145736 | tf_op jit(solution)/shard_map/while/body/eval_jaxpr/ppermute | solution.py:16
  1728.9 23.9 %collective-permute-start.1 = (bf16[2,16,128,128]{3,2,1,0:T(8,128)(2,1)}, bf16[2,16,128,128]{3,2,1,0:T(8,128)(2,1)}, u32[]{:S(2)}, u32[]{:S(2)}) collective-permute-start(bf16[2,16,128,128]{3,2,1,0:T(8,128)(2,1)} %pad_maximum_fusion.5), channel_id=1, source_target_pairs={{0,1},{1,2},{2,3},{3,4},{4,5},{5,6},{6,7},{7,8},{8,9},{9,10},{10,1... | collective-permute-start | bytes 3145736 | tf_op jit(solution)/shard_map/while/body/eval_jaxpr/ppermute | solution.py:16
  1761.6 23.0 %collective-permute-start.1 = (bf16[2,16,128,128]{3,2,1,0:T(8,128)(2,1)}, bf16[2,16,128,128]{3,2,1,0:T(8,128)(2,1)}, u32[]{:S(2)}, u32[]{:S(2)}) collective-permute-start(bf16[2,16,128,128]{3,2,1,0:T(8,128)(2,1)} %pad_maximum_fusion.5), channel_id=1, source_target_pairs={{0,1},{1,2},{2,3},{3,4},{4,5},{5,6},{6,7},{7,8},{8,9},{9,10},{10,1... | collective-permute-start | bytes 3145736 | tf_op jit(solution)/shard_map/while/body/eval_jaxpr/ppermute | solution.py:16
  1793.4 22.1 %collective-permute-start.1 = (bf16[2,16,128,128]{3,2,1,0:T(8,128)(2,1)}, bf16[2,16,128,128]{3,2,1,0:T(8,128)(2,1)}, u32[]{:S(2)}, u32[]{:S(2)}) collective-permute-start(bf16[2,16,128,128]{3,2,1,0:T(8,128)(2,1)} %pad_maximum_fusion.5), channel_id=1, source_target_pairs={{0,1},{1,2},{2,3},{3,4},{4,5},{5,6},{6,7},{7,8},{8,9},{9,10},{10,1... | collective-permute-start | bytes 3145736 | tf_op jit(solution)/shard_map/while/body/eval_jaxpr/ppermute | solution.py:16
  1824.3 21.1 %collective-permute-start.1 = (bf16[2,16,128,128]{3,2,1,0:T(8,128)(2,1)}, bf16[2,16,128,128]{3,2,1,0:T(8,128)(2,1)}, u32[]{:S(2)}, u32[]{:S(2)}) collective-permute-start(bf16[2,16,128,128]{3,2,1,0:T(8,128)(2,1)} %pad_maximum_fusion.5), channel_id=1, source_target_pairs={{0,1},{1,2},{2,3},{3,4},{4,5},{5,6},{6,7},{7,8},{8,9},{9,10},{10,1... | collective-permute-start | bytes 3145736 | tf_op jit(solution)/shard_map/while/body/eval_jaxpr/ppermute | solution.py:16
  1854.3 20.2 collective-permute-start.1
  1883.3 19.3 collective-permute-start.1
  (72 other events, 1430.2 us)
Sparse Core Ops, SparseCore 0:
  9.5 156.2 all-gather.3
  1115.4 85.1 all-reduce.2
where the time goes:
time: 2100 us; the launch traced here: 2080 us
  other arithmetic  789 us (38%)
  waiting for transfers between devices  771 us (37%)
  matrix products  326 us (16%)
  local copies, waits for them, and re-layouts  74.7 us (4%)
  starting transfers between devices  57.7 us (3%)
  blocking collectives  24.4 us (1%)
  loops' own time  23.7 us (1%)
    another operation x5, other arithmetic, block_solve(): lax.linalg.triangular_solve(system, right_side, left_side=True, lower=Tru...  632 us
    ppermute x30, waiting for transfers between devices, from_behind(): return lax.ppermute(value, axis, pairs)  629 us
    all_gather x1, waiting for transfers between devices, shards(): lax.all_gather(w_qkv[0], 'seq', axis=0, tiled=True)  130 us
    select_n x30, other arithmetic, hop_once(): return jnp.where(position == 0, empty_map, passed)  87.6 us
    dot_general x30, matrix products, compose(): jnp.einsum('hij,hjk->hik', latter[0], earlier[0], precision=FULL_PRECISION)  74.3 us
    ppermute x30, starting transfers between devices, from_behind(): return lax.ppermute(value, axis, pairs)  57.6 us
    dot_general x30, matrix products, compose(): jnp.einsum('hij,hjk->hik', latter[0], earlier[1], precision=FULL_PRECISION)  54.3 us
  transfers between devices with their start and end apart: 33, of which 32 were waited for; matrix products, arithmetic and copies ran while one was open for 20% of the time, Pallas kernels for 0%

commit v1 on v0

--- a/solution.py
+++ b/solution.py
@@ -8,6 +8,44 @@
 GROUP = 64
 TICKS = 2
 FULL_PRECISION = lax.Precision.HIGHEST
+
+
+def resolve_local_data_by_axis(row_data, dim_i):
+    row_data = jnp.moveaxis(row_data, 0, dim_i)
+    value_now = row_data.shape
+    block_out = row_data.reshape(
+        *value_now[:dim_i], value_now[dim_i] * value_now[dim_i + 1], *value_now[dim_i + 2 :]
+    )
+    return block_out
+
+
+def _trace_map(axis_k, axis_id, x_in):
+    n_lanes = lax.axis_size(axis_id)
+    windows = []
+    dd = 0
+    while dd < n_lanes:
+        windows.append((dd, (dd + 1) % n_lanes))
+        dd += 1
+    crops = []
+    for rr, pp in windows:
+        crops.append((pp, rr))
+    view_out, arr_next = ([], [])
+    dev = 0
+    while dev < n_lanes - 1:
+        if dev % 2 == 0:
+            view_out.append(
+                lax.ppermute(view_out[-1] if view_out else x_in, axis_name=axis_id, perm=windows)
+            )
+        else:
+            arr_next.append(
+                lax.ppermute(arr_next[-1] if arr_next else x_in, axis_name=axis_id, perm=crops)
+            )
+        dev = dev + 1
+    base_arr = jnp.stack([*view_out[::-1], x_in, *arr_next])
+    new = lax.axis_index(axis_id) - len(view_out)
+    base_arr = base_arr[(jnp.arange(n_lanes) - new) % n_lanes]
+    raw_out = resolve_local_data_by_axis(base_arr, axis_k)
+    return raw_out
 
 
 def from_behind(value, axis, by):
@@ -158,7 +196,7 @@
 
 def shards(residual, w_qkv, w_beta, beta_bias, norm_gain, out_gain, state_in, doc_start):
     weight_qkv, weight_beta = (
-        lax.all_gather(w_qkv[0], "seq", axis=0, tiled=True),
+        _trace_map(0, "seq", w_qkv[0]),
         lax.all_gather(w_beta[0], "seq", axis=0, tiled=True),
     )
     seq_count = lax.axis_size("seq")

time: 2100 us -> 2300 us (1.095)
  waiting for transfers between devices: 771 us -> 863 us
  local copies, waits for them, and re-layouts: 74.7 us -> 122 us
  blocking collectives: 24.4 us -> 54.6 us
  starting transfers between devices: 57.7 us -> 87.3 us
    ppermute x0 -> x15, waiting for transfers between devices: none -> 221 us  [the longest x8 220 us: _trace_map(): lax.ppermute(view_out[-1] if view_out else x_in, axis_name=axis_id, perm=...]
    all_gather x1 -> x0, waiting for transfers between devices: 130 us -> none  [shards(): lax.all_gather(w_qkv[0], 'seq', axis=0, tiled=True)]
    unnamed x38 -> x87, local copies, waits for them, and re-layouts: 8.31 us -> 39 us
    all_gather x1, blocking collectives: 24.4 us -> 54.6 us  [shards(): lax.all_gather(w_beta[0], 'seq', axis=0, tiled=True)]
    ppermute x0 -> x15, starting transfers between devices: none -> 30 us  [the longest x7 28.4 us: _trace_map(): lax.ppermute(arr_next[-1] if arr_next else x_in, axis_name=axis_id, perm=...]
  transfers between devices with their start and end apart: 33 -> 47, of which waited for: 32 -> 41; matrix products, arithmetic and copies ran while one was open for 20% -> 19% of each run, Pallas kernels for 0% -> 0%
where the time goes in v1:
time: 2300 us; the launch traced here: 2280 us
  waiting for transfers between devices  863 us (38%)
  other arithmetic  788 us (34%)
  matrix products  326 us (14%)
  local copies, waits for them, and re-layouts  122 us (5%)
  starting transfers between devices  87.3 us (4%)
  blocking collectives  54.6 us (2%)
    another operation x5, other arithmetic, block_solve(): lax.linalg.triangular_solve(system, right_side, left_side=True, lower=Tru...  632 us
    ppermute x30, waiting for transfers between devices, from_behind(): return lax.ppermute(value, axis, pairs)  630 us
    ppermute x8, waiting for transfers between devices, _trace_map(): lax.ppermute(view_out[-1] if view_out else x_in, axis_name=axis_id, perm=...  220 us
    select_n x30, other arithmetic, hop_once(): return jnp.where(position == 0, empty_map, passed)  86.3 us
    dot_general x30, matrix products, compose(): jnp.einsum('hij,hjk->hik', latter[0], earlier[0], precision=FULL_PRECISION)  74.3 us
    ppermute x30, starting transfers between devices, from_behind(): return lax.ppermute(value, axis, pairs)  57.3 us
    all_gather x1, blocking collectives, shards(): lax.all_gather(w_beta[0], 'seq', axis=0, tiled=True)  54.6 us
    dot_general x30, matrix products, compose(): jnp.einsum('hij,hjk->hik', latter[0], earlier[1], precision=FULL_PRECISION)  54.3 us
  transfers between devices with their start and end apart: 47, of which 41 were waited for; matrix products, arithmetic and copies ran while one was open for 19% of the time, Pallas kernels for 0%

profile of v1, /device:TPU:34, one launch (start us, length us, event | category | flops | bytes accessed | tf_op | source)
XLA Modules:
  0.0 2278.6 jit_solution(1218036770422288263)
XLA Ops:
  8.1 36.9 %collective-permute-done.2 = bf16[128,6144]{1,0:T(8,128)(2,1)S(1)} collective-permute-done((bf16[128,6144]{1,0:T(8,128)(2,1)}, bf16[128,6144]{1,0:T(8,128)(2,1)S(1)}, u32[]{:S(2)}, u32[]{:S(2)}) %collective-permute-start.2) | collective-permute-done | bytes 1572896 | tf_op jit(solution)/shard_map/ppermute | solution.py:37
  50.3 33.2 %collective-permute-done.3 = bf16[128,6144]{1,0:T(8,128)(2,1)S(1)} collective-permute-done((bf16[128,6144]{1,0:T(8,128)(2,1)S(1)}, bf16[128,6144]{1,0:T(8,128)(2,1)S(1)}, u32[]{:S(2)}, u32[]{:S(2)}) %collective-permute-start.3) | collective-permute-done | bytes 1572896 | tf_op jit(solution)/shard_map/ppermute | solution.py:37
  88.8 31.2 %collective-permute-done.4 = bf16[128,6144]{1,0:T(8,128)(2,1)S(1)} collective-permute-done((bf16[128,6144]{1,0:T(8,128)(2,1)S(1)}, bf16[128,6144]{1,0:T(8,128)(2,1)S(1)}, u32[]{:S(2)}, u32[]{:S(2)}) %collective-permute-start.4) | collective-permute-done | bytes 1572896 | tf_op jit(solution)/shard_map/ppermute | solution.py:37
  125.0 30.5 %collective-permute-done.5 = bf16[128,6144]{1,0:T(8,128)(2,1)S(1)} collective-permute-done((bf16[128,6144]{1,0:T(8,128)(2,1)S(1)}, bf16[128,6144]{1,0:T(8,128)(2,1)S(1)}, u32[]{:S(2)}, u32[]{:S(2)}) %collective-permute-start.5) | collective-permute-done | bytes 1572896 | tf_op jit(solution)/shard_map/ppermute | solution.py:37
  160.2 29.9 %collective-permute-done.6 = bf16[128,6144]{1,0:T(8,128)(2,1)S(1)} collective-permute-done((bf16[128,6144]{1,0:T(8,128)(2,1)S(1)}, bf16[128,6144]{1,0:T(8,128)(2,1)S(1)}, u32[]{:S(2)}, u32[]{:S(2)}) %collective-permute-start.6) | collective-permute-done | bytes 1572896 | tf_op jit(solution)/shard_map/ppermute | solution.py:37
  194.8 29.9 %collective-permute-done.7 = bf16[128,6144]{1,0:T(8,128)(2,1)S(1)} collective-permute-done((bf16[128,6144]{1,0:T(8,128)(2,1)S(1)}, bf16[128,6144]{1,0:T(8,128)(2,1)S(1)}, u32[]{:S(2)}, u32[]{:S(2)}) %collective-permute-start.7) | collective-permute-done | bytes 1572896 | tf_op jit(solution)/shard_map/ppermute | solution.py:37
  230.4 28.6 %collective-permute-done.8 = bf16[128,6144]{1,0:T(8,128)(2,1)} collective-permute-done((bf16[128,6144]{1,0:T(8,128)(2,1)S(1)}, bf16[128,6144]{1,0:T(8,128)(2,1)}, u32[]{:S(2)}, u32[]{:S(2)}) %collective-permute-start.8) | collective-permute-done | bytes 1572896 | tf_op jit(solution)/shard_map/ppermute | solution.py:37
  259.1 54.6 %all-gather = bf16[1,2048,16]{1,2,0:T(8,128)(2,1)S(1)} all-gather(bf16[1,128,16]{1,2,0:T(8,128)(2,1)} %param.24), channel_id=2, replica_groups=mesh['section'=8,'seq'=16] {'seq'}, dimensions={1}, use_global_device_ids=true | all-gather | bytes 69632 | tf_op jit(solution)/shard_map/all_gather | solution.py:200
  373.4 32.9 %copy.59 = bf16[6144,2048]{1,0:T(8,128)(2,1)} copy(bf16[6144,2048]{0,1:T(8,128)(2,1)} %bitcast.384) | data formatting | bytes 50331648 | tf_op jit(solution)/shard_map/dot_general | solution.py:93
  428.6 316.0 %custom-call.6 = f32[4,16,1,64,64]{3,4,2,1,0:T(8,128)} custom-call(f32[4,16,1,64,64]{4,3,2,1,0:T(8,128)} %add_bitcast_fusion.1), custom_call_target="InvertDiagBlocksLowerTriangular" | custom-call | tf_op jit(solution)/shard_map/triangular_solve/custom-call.1 | solution.py:80
  753.9 41.5 %while.80 = (s32[]{:T(128)}, f32[16,128,128]{2,1,0:T(8,128)S(1)}, f32[16,128,128]{2,1,0:T(8,128)S(1)}, s32[4]{0:T(128)S(1)}, s32[]{:T(128)}, /*index=5*/f32[4,16...) while((s32[]{:T(128)}, f32[16,128,128]{2,1,0:T(8,128)S(1)}, ...), condition=%wide.region_3.5_spmd.clone, body=%wide.region_2.4_spmd.clone.sunk | while | flops 807534592 | bytes 19400364 | solution.py:171
  798.4 465.0 %while.76 = (s32[]{:T(128)}, f32[2,16,128,128]{3,2,1,0:T(8,128)}, pred[]{:T(512)}, f32[16,128,128]{2,1,0:T(8,128)S(1)}, f32[16,128,128]{2,1,0:T(8,128)S(1)}, /*index=5*/f32[2,16,128,128]{3,2,1,0:T(8,128)}, s32[]{:T(128)}) while((s32[]{:T(128)}, f32[2,16,128,128]{3,2,1,0:T(8,128)}, pred[]{:T(512)}, f32[16,128,128]{2,1,0:T(8,128)S(1)}, ...), condition=%wide.region_5.7_spmd, body=%wide.region_4.6_spmd.sunk | while | flops 807665664 | bytes 26214544 | solution.py:225
  1098.0 25.0 %collective-permute-done = bf16[2,16,128,128]{3,2,1,0:T(8,128)(2,1)} collective-permute-done((bf16[2,16,128,128]{3,2,1,0:T(8,128)(2,1)}, bf16[2,16,128,128]{3,2,1,0:T(8,128)(2,1)}, u32[]{:S(2)}, u32[]{:S(2)}) %collective-permute-start) | collective-permute-done | bytes 1048608 | tf_op jit(solution)/shard_map/while/body/eval_jaxpr/ppermute | solution.py:54
  1132.7 26.0 %collective-permute-done = bf16[2,16,128,128]{3,2,1,0:T(8,128)(2,1)} collective-permute-done((bf16[2,16,128,128]{3,2,1,0:T(8,128)(2,1)}, bf16[2,16,128,128]{3,2,1,0:T(8,128)(2,1)}, u32[]{:S(2)}, u32[]{:S(2)}) %collective-permute-start) | collective-permute-done | bytes 1048608 | tf_op jit(solution)/shard_map/while/body/eval_jaxpr/ppermute | solution.py:54
  1168.4 27.2 %collective-permute-done = bf16[2,16,128,128]{3,2,1,0:T(8,128)(2,1)} collective-permute-done((bf16[2,16,128,128]{3,2,1,0:T(8,128)(2,1)}, bf16[2,16,128,128]{3,2,1,0:T(8,128)(2,1)}, u32[]{:S(2)}, u32[]{:S(2)}) %collective-permute-start) | collective-permute-done | bytes 1048608 | tf_op jit(solution)/shard_map/while/body/eval_jaxpr/ppermute | solution.py:54
  1205.2 28.3 %collective-permute-done = bf16[2,16,128,128]{3,2,1,0:T(8,128)(2,1)} collective-permute-done((bf16[2,16,128,128]{3,2,1,0:T(8,128)(2,1)}, bf16[2,16,128,128]{3,2,1,0:T(8,128)(2,1)}, u32[]{:S(2)}, u32[]{:S(2)}) %collective-permute-start) | collective-permute-done | bytes 1048608 | tf_op jit(solution)/shard_map/while/body/eval_jaxpr/ppermute | solution.py:54
  1267.7 47.7 %while.78 = (s32[]{:T(128)}, f32[16,128,128]{2,1,0:T(8,128)S(1)}, f32[4,16,64,128]{3,2,1,0:T(8,128)}, s32[4]{0:T(128)S(1)}, s32[]{:T(128)}, /*index=5*/f32[4,16,...) while((s32[]{:T(128)}, f32[16,128,128]{2,1,0:T(8,128)S(1)}, ...), condition=%wide.region_8.10_spmd.clone, body=%wide.region_7.9_spmd.clone.sunk | while | flops 806690816 | bytes 19451036 | solution.py:138
  1366.6 316.0 %custom-call.7 = f32[4,16,1,64,64]{3,4,2,1,0:T(8,128)} custom-call(f32[4,16,1,64,64]{4,3,2,1,0:T(8,128)} %add_bitcast_fusion), custom_call_target="InvertDiagBlocksLowerTriangular" | custom-call | tf_op jit(solution)/shard_map/triangular_solve/custom-call.1 | solution.py:80
  1691.9 54.5 %while.81 = (s32[]{:T(128)}, f32[16,128,128]{2,1,0:T(8,128)S(1)}, f32[16,128,128]{2,1,0:T(8,128)}, s32[4]{0:T(128)S(1)}, s32[]{:T(128)}, /*index=5*/f32[4,16,64,...) while((s32[]{:T(128)}, f32[16,128,128]{2,1,0:T(8,128)S(1)}, ...), condition=%wide.region_13.15_spmd.clone, body=%wide.region_12.14_spmd.clone.sunk | while | flops 807534592 | bytes 19401408 | solution.py:171
  1749.4 470.7 %while.77 = (s32[]{:T(128)}, f32[2,16,128,128]{3,2,1,0:T(8,128)}, pred[]{:T(512)}, f32[16,128,128]{2,1,0:T(8,128)S(1)}, f32[16,128,128]{2,1,0:T(8,128)}, /*index=5*/f32[2,16,128,128]{3,2,1,0:T(8,128)S(1)}, s32[]{:T(128)}) while((s32[]{:T(128)}, f32[2,16,128,128]{3,2,1,0:T(8,128)}, pred[]{:T(512)}, f32[16,128,128]{2,1,0:T(8,128)S(1)}, ...), condition=%wide.region_15.17_spmd, body=%wide.region_14.16_spmd.sunk | while | flops 807665664 | bytes 22020240 | solution.py:225
  1757.3 26.6 %collective-permute-done.1 = bf16[2,16,128,128]{3,2,1,0:T(8,128)(2,1)} collective-permute-done((bf16[2,16,128,128]{3,2,1,0:T(8,128)(2,1)}, bf16[2,16,128,128]{3,2,1,0:T(8,128)(2,1)}, u32[]{:S(2)}, u32[]{:S(2)}) %collective-permute-start.1) | collective-permute-done | bytes 1048608 | tf_op jit(solution)/shard_map/while/body/eval_jaxpr/ppermute | solution.py:54
  1794.5 25.7 %collective-permute-done.1 = bf16[2,16,128,128]{3,2,1,0:T(8,128)(2,1)} collective-permute-done((bf16[2,16,128,128]{3,2,1,0:T(8,128)(2,1)}, bf16[2,16,128,128]{3,2,1,0:T(8,128)(2,1)}, u32[]{:S(2)}, u32[]{:S(2)}) %collective-permute-start.1) | collective-permute-done | bytes 1048608 | tf_op jit(solution)/shard_map/while/body/eval_jaxpr/ppermute | solution.py:54
  1830.9 24.8 %collective-permute-done.1 = bf16[2,16,128,128]{3,2,1,0:T(8,128)(2,1)} collective-permute-done((bf16[2,16,128,128]{3,2,1,0:T(8,128)(2,1)}, bf16[2,16,128,128]{3,2,1,0:T(8,128)(2,1)}, u32[]{:S(2)}, u32[]{:S(2)}) %collective-permute-start.1) | collective-permute-done | bytes 1048608 | tf_op jit(solution)/shard_map/while/body/eval_jaxpr/ppermute | solution.py:54
  2224.1 39.2 %while.79 = (s32[]{:T(128)}, f32[16,128,128]{2,1,0:T(8,128)S(1)}, f32[4,16,64,128]{3,2,1,0:T(8,128)}, s32[4]{0:T(128)S(1)}, s32[]{:T(128)}, /*index=5*/f32[4,16,...) while((s32[]{:T(128)}, f32[16,128,128]{2,1,0:T(8,128)S(1)}, ...), condition=%wide.region_19.21_spmd.clone, body=%wide.region_18.20_spmd.clone.sunk | while | flops 806690816 | bytes 19451036 | solution.py:138
  (557 shorter events, 1118.8 us)
Async XLA Ops:
  6.5 1742.9 %all-reduce.3.cloned.1.call-start = ((), (), s32[]{:S(2)}) async-start(), calls=%async_computation | async-start | bytes 1048576 | tf_op jit(solution)/shard_map/psum | solution.py:59
  6.5 38.5 %collective-permute-start.2 = (bf16[128,6144]{1,0:T(8,128)(2,1)}, bf16[128,6144]{1,0:T(8,128)(2,1)S(1)}, u32[]{:S(2)}, u32[]{:S(2)}) collective-permute-start(bf16[128,6144]{1,0:T(8,128)(2,1)} %bitcast.399), channel_id=1, source_target_pairs={{0,1},{1,2},{2,3},{3,4},{4,5},{5,6},{6,7},{7,8},{8,9},{9,10},{10,1... | collective-permute-start | bytes 4718600 | tf_op jit(solution)/shard_map/ppermute | solution.py:37
  46.1 37.4 %collective-permute-start.3 = (bf16[128,6144]{1,0:T(8,128)(2,1)S(1)}, bf16[128,6144]{1,0:T(8,128)(2,1)S(1)}, u32[]{:S(2)}, u32[]{:S(2)}) collective-permute-start(bf16[128,6144]{1,0:T(8,128)(2,1)S(1)} %collective-permute-done.2), channel_id=1, source_target_pairs={{0,1},{1,2},{2,3},{3,4},{4,5},{5,6},{6,7},{7,8},{8,9},{9,10},{10,1... | collective-permute-start | bytes 4718600 | tf_op jit(solution)/shard_map/ppermute | solution.py:37
  46.1 37.4 %collective-permute-start.10 = (bf16[128,6144]{1,0:T(8,128)(2,1)}, bf16[128,6144]{1,0:T(8,128)(2,1)S(1)}, u32[]{:S(2)}, u32[]{:S(2)}) collective-permute-start(bf16[128,6144]{1,0:T(8,128)(2,1)} %bitcast.400), channel_id=1, source_target_pairs={{1,0},{2,1},{3,2},{4,3},{5,4},{6,5},{7,6},{8,7},{9,8},{10,9},{11,1... | collective-permute-start | bytes 4718600 | tf_op jit(solution)/shard_map/ppermute | solution.py:41
  83.5 36.5 %collective-permute-start.4 = (bf16[128,6144]{1,0:T(8,128)(2,1)S(1)}, bf16[128,6144]{1,0:T(8,128)(2,1)S(1)}, u32[]{:S(2)}, u32[]{:S(2)}) collective-permute-start(bf16[128,6144]{1,0:T(8,128)(2,1)S(1)} %collective-permute-done.3), channel_id=1, source_target_pairs={{0,1},{1,2},{2,3},{3,4},{4,5},{5,6},{6,7},{7,8},{8,9},{9,10},{10,1... | collective-permute-start | bytes 4718600 | tf_op jit(solution)/shard_map/ppermute | solution.py:37
  84.7 35.7 %collective-permute-start.11 = (bf16[128,6144]{1,0:T(8,128)(2,1)S(1)}, bf16[128,6144]{1,0:T(8,128)(2,1)S(1)}, u32[]{:S(2)}, u32[]{:S(2)}) collective-permute-start(bf16[128,6144]{1,0:T(8,128)(2,1)S(1)} %collective-permute-done.10), channel_id=1, source_target_pairs={{1,0},{2,1},{3,2},{4,3},{5,4},{6,5},{7,6},{8,7},{9,8},{10,9},{11,1... | collective-permute-start | bytes 4718600 | tf_op jit(solution)/shard_map/ppermute | solution.py:41
  120.0 35.5 %collective-permute-start.5 = (bf16[128,6144]{1,0:T(8,128)(2,1)S(1)}, bf16[128,6144]{1,0:T(8,128)(2,1)S(1)}, u32[]{:S(2)}, u32[]{:S(2)}) collective-permute-start(bf16[128,6144]{1,0:T(8,128)(2,1)S(1)} %collective-permute-done.4), channel_id=1, source_target_pairs={{0,1},{1,2},{2,3},{3,4},{4,5},{5,6},{6,7},{7,8},{8,9},{9,10},{10,1... | collective-permute-start | bytes 4718600 | tf_op jit(solution)/shard_map/ppermute | solution.py:37
  120.4 35.2 %collective-permute-start.12 = (bf16[128,6144]{1,0:T(8,128)(2,1)S(1)}, bf16[128,6144]{1,0:T(8,128)(2,1)S(1)}, u32[]{:S(2)}, u32[]{:S(2)}) collective-permute-start(bf16[128,6144]{1,0:T(8,128)(2,1)S(1)} %collective-permute-done.11), channel_id=1, source_target_pairs={{1,0},{2,1},{3,2},{4,3},{5,4},{6,5},{7,6},{8,7},{9,8},{10,9},{11,1... | collective-permute-start | bytes 4718600 | tf_op jit(solution)/shard_map/ppermute | solution.py:41
  155.5 34.6 %collective-permute-start.6 = (bf16[128,6144]{1,0:T(8,128)(2,1)S(1)}, bf16[128,6144]{1,0:T(8,128)(2,1)S(1)}, u32[]{:S(2)}, u32[]{:S(2)}) collective-permute-start(bf16[128,6144]{1,0:T(8,128)(2,1)S(1)} %collective-permute-done.5), channel_id=1, source_target_pairs={{0,1},{1,2},{2,3},{3,4},{4,5},{5,6},{6,7},{7,8},{8,9},{9,10},{10,1... | collective-permute-start | bytes 4718600 | tf_op jit(solution)/shard_map/ppermute | solution.py:37
  155.6 34.6 %collective-permute-start.13 = (bf16[128,6144]{1,0:T(8,128)(2,1)S(1)}, bf16[128,6144]{1,0:T(8,128)(2,1)S(1)}, u32[]{:S(2)}, u32[]{:S(2)}) collective-permute-start(bf16[128,6144]{1,0:T(8,128)(2,1)S(1)} %collective-permute-done.12), channel_id=1, source_target_pairs={{1,0},{2,1},{3,2},{4,3},{5,4},{6,5},{7,6},{8,7},{9,8},{10,9},{11,1... | collective-permute-start | bytes 4718600 | tf_op jit(solution)/shard_map/ppermute | solution.py:41
  190.1 34.6 %collective-permute-start.7 = (bf16[128,6144]{1,0:T(8,128)(2,1)S(1)}, bf16[128,6144]{1,0:T(8,128)(2,1)S(1)}, u32[]{:S(2)}, u32[]{:S(2)}) collective-permute-start(bf16[128,6144]{1,0:T(8,128)(2,1)S(1)} %collective-permute-done.6), channel_id=1, source_target_pairs={{0,1},{1,2},{2,3},{3,4},{4,5},{5,6},{6,7},{7,8},{8,9},{9,10},{10,1... | collective-permute-start | bytes 4718600 | tf_op jit(solution)/shard_map/ppermute | solution.py:37
  190.2 36.6 %collective-permute-start.14 = (bf16[128,6144]{1,0:T(8,128)(2,1)S(1)}, bf16[128,6144]{1,0:T(8,128)(2,1)}, u32[]{:S(2)}, u32[]{:S(2)}) collective-permute-start(bf16[128,6144]{1,0:T(8,128)(2,1)S(1)} %collective-permute-done.13), channel_id=1, source_target_pairs={{1,0},{2,1},{3,2},{4,3},{5,4},{6,5},{7,6},{8,7},{9,8},{10,9},{11,1... | collective-permute-start | bytes 4718600 | tf_op jit(solution)/shard_map/ppermute | solution.py:41
  224.7 34.4 %collective-permute-start.8 = (bf16[128,6144]{1,0:T(8,128)(2,1)S(1)}, bf16[128,6144]{1,0:T(8,128)(2,1)}, u32[]{:S(2)}, u32[]{:S(2)}) collective-permute-start(bf16[128,6144]{1,0:T(8,128)(2,1)S(1)} %collective-permute-done.7), channel_id=1, source_target_pairs={{0,1},{1,2},{2,3},{3,4},{4,5},{5,6},{6,7},{7,8},{8,9},{9,10},{10,1... | collective-permute-start | bytes 4718600 | tf_op jit(solution)/shard_map/ppermute | solution.py:37
  226.7 91.8 %collective-permute-start.15 = (bf16[128,6144]{1,0:T(8,128)(2,1)}, bf16[128,6144]{1,0:T(8,128)(2,1)}, u32[]{:S(2)}, u32[]{:S(2)}) collective-permute-start(bf16[128,6144]{1,0:T(8,128)(2,1)} %collective-permute-done.14), channel_id=1, source_target_pairs={{1,0},{2,1},{3,2},{4,3},{5,4},{6,5},{7,6},{8,7},{9,8},{10,9},{11,1... | collective-permute-start | bytes 4718600 | tf_op jit(solution)/shard_map/ppermute | solution.py:41
  259.0 62.3 %collective-permute-start.9 = (bf16[128,6144]{1,0:T(8,128)(2,1)}, bf16[128,6144]{1,0:T(8,128)(2,1)}, u32[]{:S(2)}, u32[]{:S(2)}) collective-permute-start(bf16[128,6144]{1,0:T(8,128)(2,1)} %collective-permute-done.8), channel_id=1, source_target_pairs={{0,1},{1,2},{2,3},{3,4},{4,5},{5,6},{6,7},{7,8},{8,9},{9,10},{10,1... | collective-permute-start | bytes 4718600 | tf_op jit(solution)/shard_map/ppermute | solution.py:37
  318.5 34.8 %collective-permute-start.16 = (bf16[128,6144]{1,0:T(8,128)(2,1)}, bf16[128,6144]{1,0:T(8,128)(2,1)S(1)}, u32[]{:S(2)}, u32[]{:S(2)}) collective-permute-start(bf16[128,6144]{1,0:T(8,128)(2,1)} %collective-permute-done.15), channel_id=1, source_target_pairs={{1,0},{2,1},{3,2},{4,3},{5,4},{6,5},{7,6},{8,7},{9,8},{10,9},{11,1... | collective-permute-start | bytes 4718600 | tf_op jit(solution)/shard_map/ppermute | solution.py:41
  1062.5 25.8 %collective-permute-start = (bf16[2,16,128,128]{3,2,1,0:T(8,128)(2,1)}, bf16[2,16,128,128]{3,2,1,0:T(8,128)(2,1)}, u32[]{:S(2)}, u32[]{:S(2)}) collective-permute-start(bf16[2,16,128,128]{3,2,1,0:T(8,128)(2,1)} %pad_maximum_fusion.4), channel_id=1, source_target_pairs={{0,1},{1,2},{2,3},{3,4},{4,5},{5,6},{6,7},{7,8},{8,9},{9,10},{10,1... | collective-permute-start | bytes 3145736 | tf_op jit(solution)/shard_map/while/body/eval_jaxpr/ppermute | solution.py:54
  1096.1 26.9 %collective-permute-start = (bf16[2,16,128,128]{3,2,1,0:T(8,128)(2,1)}, bf16[2,16,128,128]{3,2,1,0:T(8,128)(2,1)}, u32[]{:S(2)}, u32[]{:S(2)}) collective-permute-start(bf16[2,16,128,128]{3,2,1,0:T(8,128)(2,1)} %pad_maximum_fusion.4), channel_id=1, source_target_pairs={{0,1},{1,2},{2,3},{3,4},{4,5},{5,6},{6,7},{7,8},{8,9},{9,10},{10,1... | collective-permute-start | bytes 3145736 | tf_op jit(solution)/shard_map/while/body/eval_jaxpr/ppermute | solution.py:54
  1130.7 28.0 %collective-permute-start = (bf16[2,16,128,128]{3,2,1,0:T(8,128)(2,1)}, bf16[2,16,128,128]{3,2,1,0:T(8,128)(2,1)}, u32[]{:S(2)}, u32[]{:S(2)}) collective-permute-start(bf16[2,16,128,128]{3,2,1,0:T(8,128)(2,1)} %pad_maximum_fusion.4), channel_id=1, source_target_pairs={{0,1},{1,2},{2,3},{3,4},{4,5},{5,6},{6,7},{7,8},{8,9},{9,10},{10,1... | collective-permute-start | bytes 3145736 | tf_op jit(solution)/shard_map/while/body/eval_jaxpr/ppermute | solution.py:54
  1166.5 29.1 %collective-permute-start = (bf16[2,16,128,128]{3,2,1,0:T(8,128)(2,1)}, bf16[2,16,128,128]{3,2,1,0:T(8,128)(2,1)}, u32[]{:S(2)}, u32[]{:S(2)}) collective-permute-start(bf16[2,16,128,128]{3,2,1,0:T(8,128)(2,1)} %pad_maximum_fusion.4), channel_id=1, source_target_pairs={{0,1},{1,2},{2,3},{3,4},{4,5},{5,6},{6,7},{7,8},{8,9},{9,10},{10,1... | collective-permute-start | bytes 3145736 | tf_op jit(solution)/shard_map/while/body/eval_jaxpr/ppermute | solution.py:54
  1203.3 30.2 %collective-permute-start = (bf16[2,16,128,128]{3,2,1,0:T(8,128)(2,1)}, bf16[2,16,128,128]{3,2,1,0:T(8,128)(2,1)}, u32[]{:S(2)}, u32[]{:S(2)}) collective-permute-start(bf16[2,16,128,128]{3,2,1,0:T(8,128)(2,1)} %pad_maximum_fusion.4), channel_id=1, source_target_pairs={{0,1},{1,2},{2,3},{3,4},{4,5},{5,6},{6,7},{7,8},{8,9},{9,10},{10,1... | collective-permute-start | bytes 3145736 | tf_op jit(solution)/shard_map/while/body/eval_jaxpr/ppermute | solution.py:54
  1755.4 28.5 %collective-permute-start.1 = (bf16[2,16,128,128]{3,2,1,0:T(8,128)(2,1)}, bf16[2,16,128,128]{3,2,1,0:T(8,128)(2,1)}, u32[]{:S(2)}, u32[]{:S(2)}) collective-permute-start(bf16[2,16,128,128]{3,2,1,0:T(8,128)(2,1)} %pad_maximum_fusion.5), channel_id=1, source_target_pairs={{0,1},{1,2},{2,3},{3,4},{4,5},{5,6},{6,7},{7,8},{8,9},{9,10},{10,1... | collective-permute-start | bytes 3145736 | tf_op jit(solution)/shard_map/while/body/eval_jaxpr/ppermute | solution.py:54
  1792.6 27.6 %collective-permute-start.1 = (bf16[2,16,128,128]{3,2,1,0:T(8,128)(2,1)}, bf16[2,16,128,128]{3,2,1,0:T(8,128)(2,1)}, u32[]{:S(2)}, u32[]{:S(2)}) collective-permute-start(bf16[2,16,128,128]{3,2,1,0:T(8,128)(2,1)} %pad_maximum_fusion.5), channel_id=1, source_target_pairs={{0,1},{1,2},{2,3},{3,4},{4,5},{5,6},{6,7},{7,8},{8,9},{9,10},{10,1... | collective-permute-start | bytes 3145736 | tf_op jit(solution)/shard_map/while/body/eval_jaxpr/ppermute | solution.py:54
  1829.0 26.7 %collective-permute-start.1 = (bf16[2,16,128,128]{3,2,1,0:T(8,128)(2,1)}, bf16[2,16,128,128]{3,2,1,0:T(8,128)(2,1)}, u32[]{:S(2)}, u32[]{:S(2)}) collective-permute-start(bf16[2,16,128,128]{3,2,1,0:T(8,128)(2,1)} %pad_maximum_fusion.5), channel_id=1, source_target_pairs={{0,1},{1,2},{2,3},{3,4},{4,5},{5,6},{6,7},{7,8},{8,9},{9,10},{10,1... | collective-permute-start | bytes 3145736 | tf_op jit(solution)/shard_map/while/body/eval_jaxpr/ppermute | solution.py:54
  (108 other events, 2199.8 us)
Sparse Core Ops, SparseCore 0:
  1327.7 90.4 all-reduce.2
